TPU v7x, 512 devices: a whole 4x8x8 slice. The times are simulated.
512 devices in a mesh: dp: 32 (over x, y), seq: 16 (over z, core).
Axes of the slice: x: 4, y: 8, z: 8, core: 2. Of those that a mesh axis runs over, the one named last changes fastest.
Arguments:
- residual_stream: bfloat16 [262144, 2048], P(('dp', 'seq')), parts along dimension 0, may hold values from -6 to 6
- octet_readout: bfloat16 [256, 2048], replicated, may hold values from -6 to 6
- downsampling_filter: bfloat16 [32, 256, 96], replicated, may hold values from -0.375 to 0.375
- sharpness_factor: float32 [8], replicated, may hold values from 4 to 20
- widening_filter: bfloat16 [32, 32, 256], replicated, may hold values from -2 to 2
Outputs:
- logits: bfloat16 [262144, 256], P(('dp', 'seq')), parts along dimension 0
There are 32 independent parts, one for each index of `dp`. A program takes and returns all parts, laid end to end along the dimension named above; an argument that names none is the same for every part. Nothing has to cross between parts.
All inputs are finite; a program needn't handle non-finite values.
Results may differ from a plain program's by a relative error of at most 0.0052.
Values may be sent and summed in bfloat16 or wider, within the bound.
A program may use at most 64 MiB of HBM per device.

v0:
```python
import jax
import jax.numpy as jnp
from jax import lax
from jax.sharding import PartitionSpec as P

SHORTEN = 4


def shifted_2(array, axis, by):
    count = lax.axis_size(axis)
    pairs = [(i, i + by) for i in range(count) if 0 <= i + by < count]
    return lax.ppermute(array, axis, pairs)


def passed_along(block, axis, distance):
    devices = range(lax.axis_size(axis))
    route = [((i - distance) % len(devices), i) for i in devices]
    return lax.ppermute(block, axis, route)


def normalize(vectors):
    return vectors * lax.rsqrt(jnp.sum(vectors * vectors, axis=-1, keepdims=True) + 1e-06)


def shorten(shifted, kernel_part, groups):
    byte_rows, model_width = shifted.shape
    windows = shifted.reshape(byte_rows // SHORTEN, SHORTEN, groups, model_width // groups)
    kernel = kernel_part.reshape(groups, SHORTEN, model_width // groups, kernel_part.shape[2])
    return jnp.einsum("jtgc,gtco->jgo", windows, kernel, preferred_element_type=jnp.float32)


def on_device(
    residual_stream, octet_readout, downsampling_filter, sharpness_factor, widening_filter
):
    byte_rows = residual_stream.shape[0]
    model_width = residual_stream.shape[1]
    groups = downsampling_filter.shape[0]
    group_width = model_width // groups
    per_group = downsampling_filter.shape[2] // 3
    attention_number = sharpness_factor.shape[0]
    head_size = groups * per_group // attention_number
    tokens_here = byte_rows // SHORTEN
    rim_rows = SHORTEN - 1
    left_rim = shifted_2(residual_stream[byte_rows - rim_rows :], "seq", 1)
    shifted = jnp.concatenate([left_rim, residual_stream[: byte_rows - rim_rows]], 0)
    mixed_out = shorten(shifted, downsampling_filter, groups)
    queries = normalize(
        mixed_out[:, :, :per_group].reshape(tokens_here, attention_number, head_size)
    ).astype(jnp.bfloat16)
    key_unit = normalize(
        mixed_out[:, :, per_group : 2 * per_group].reshape(tokens_here, attention_number, head_size)
    ).astype(jnp.bfloat16)
    values = (
        mixed_out[:, :, 2 * per_group :]
        .reshape(tokens_here, attention_number, head_size)
        .astype(jnp.bfloat16)
    )
    my_index = lax.axis_index("seq")
    first_token = my_index * tokens_here
    sharpness_vertical = sharpness_factor[:, None, None]
    query_pos = first_token + jnp.arange(tokens_here, dtype=jnp.int32)
    stacked = jnp.stack([key_unit, values], 0)
    gathered = lax.all_gather(stacked, "seq", axis=1, tiled=True)
    all_keys, all_values = (gathered[0], gathered[1])
    similarity_matrix = (
        jnp.einsum("jsg,isg->sji", queries, all_keys, preferred_element_type=jnp.float32)
        * sharpness_vertical
    )
    key_pos = jnp.arange(all_keys.shape[0], dtype=jnp.int32)
    future_masked = key_pos[None, :] <= query_pos[:, None]
    softmax_shares = jnp.where(
        future_masked[None],
        jnp.exp(similarity_matrix - sharpness_vertical),
        jnp.zeros((), jnp.float32),
    )
    denom_sum = jnp.sum(softmax_shares, axis=-1)
    weighted = jnp.einsum(
        "hqk,khd->qhd",
        softmax_shares.astype(jnp.bfloat16),
        all_values,
        preferred_element_type=jnp.float32,
    )
    attended = (weighted / jnp.transpose(denom_sum)[:, :, None]).astype(jnp.bfloat16)
    attended = attended.reshape(tokens_here, groups, per_group)
    upsampled = jnp.einsum(
        "jgc,gcu->jgu", attended, widening_filter, preferred_element_type=jnp.float32
    )
    upsampled = (
        upsampled.reshape(tokens_here, groups, SHORTEN, group_width)
        .transpose(0, 2, 1, 3)
        .reshape(byte_rows, model_width)
    )
    hidden = residual_stream.astype(jnp.float32) + upsampled
    normed = (hidden * lax.rsqrt(jnp.mean(hidden * hidden, axis=-1, keepdims=True) + 1e-05)).astype(
        jnp.bfloat16
    )
    logits = lax.dot_general(
        normed, octet_readout, (((1,), (1,)), ((), ())), preferred_element_type=jnp.float32
    ) * model_width ** (-0.5)
    return logits.astype(jnp.bfloat16)


def solution(mesh):
    in_specs = (P(("dp", "seq"), None), P(), P(), P(), P())
    out_specs = P(("dp", "seq"), None)
    return jax.shard_map(
        on_device, mesh=mesh, in_specs=in_specs, out_specs=out_specs, check_vma=False
    )
```

profile of v0, /device:TPU:1, one launch (start us, length us, event | category | flops | bytes accessed | tf_op | source)
XLA Modules:
  0.0 155.1 jit_solution(6165816291397608881)
XLA Ops:
  6.5 0.0 copy-start
  6.5 0.0 copy-start.2
  6.5 0.0 all-gather.2.cloned.1.call-start
  6.5 0.9 slice.22
  7.5 5.5 %collective-permute-start = (bf16[3,2048]{1,0:T(4,128)(2,1)S(1)}, bf16[3,2048]{1,0:T(4,128)(2,1)S(1)}, u32[]{:S(2)}, u32[]{:S(2)}) collective-permute-start(bf16[3,2048]{1,0:T(4,128)(2,1)S(1)} %slice.22), channel_id=1, source_target_pairs={{0,1},{1,2},{2,3},{3,4},{4,5},{5,6},{6,7},{7,8},{8,9},{9,10},{10,1... | collective-permute-start | bytes 36872 | tf_op jit(solution)/shard_map/ppermute | solution.py:12
  13.0 3.9 %copy.12 = bf16[32,256,96]{2,1,0:T(8,128)(2,1)} copy(bf16[32,256,96]{1,2,0:T(8,128)(2,1)} %param.7) | data formatting | bytes 3145728 | tf_op args[2]
  16.8 0.0 collective-permute-done
  16.8 0.0 copy-done.2
  16.9 1.9 %pad_maximum_fusion = bf16[512,2048]{1,0:T(8,128)(2,1)} fusion(bf16[509,2048]{1,0:T(8,128)(2,1)S(1)} %bitcast.45, bf16[3,2048]{1,0:T(4,128)(2,1)S(1)} %collective-permute-done), kind=kLoop, calls=%fused_computation.17 | loop fusion | flops 4194304 | bytes 4194304 | tf_op jit(solution)/shard_map/concatenate | solution.py:45
  18.8 7.1 %reshape.93 = bf16[128,4,32,64]{3,2,1,0:T(8,128)(2,1)} reshape(bf16[512,2048]{1,0:T(8,128)(2,1)} %pad_maximum_fusion) | data formatting | bytes 4194304 | tf_op jit(solution)/shard_map/reshape | solution.py:27
  25.9 7.8 %fusion.12 = f32[128,32,96]{0,2,1:T(8,128)S(1)} fusion(bf16[32,4,64,96]{3,2,1,0:T(8,128)(2,1)} %bitcast.47, bf16[128,4,32,64]{3,2,1,0:T(8,128)(2,1)} %reshape.93), kind=kOutput, calls=%fused_computation.19 | convolution fusion | flops 201326592 | bytes 5242880 | tf_op jit(solution)/shard_map/jtgc,gtco->jgo/dot_general | solution.py:29
  33.7 0.0 copy-start.5
  33.7 1.1 multiply_reduce_fusion.1
  34.9 0.9 copy.15
  35.7 2.1 %copy.14 = f32[1,128,8,128]{3,1,2,0:T(8,128)} copy(f32[1,128,8,128]{1,3,2,0:T(8,128)} %bitcast.49) | data formatting | bytes 1048576 | tf_op jit(solution)/shard_map/reshape | solution.py:51
  37.8 1.2 multiply_convert_fusion.7
  39.0 1.9 %pad_maximum_fusion.1 = bf16[2,128,8,128]{3,1,2,0:T(8,128)(2,1)} fusion(bf16[1,128,8,128]{3,1,2,0:T(8,128)(2,1)} %copy.15, bf16[1,128,8,128]{3,1,2,0:T(8,128)(2,1)S(1)} %multiply_convert_fusion.7), kind=kLoop, calls=%fused_computation.27 | loop fusion | flops 262144 | bytes 1048576 | tf_op jit(solution)/shard_map/stack | solution.py:62
  40.9 0.0 all-gather.2.cloned.1.call-update
  40.9 0.2 iota_compare_fusion
  41.2 2.0 %copy.16 = f32[128,8,128]{2,0,1:T(8,128)} copy(f32[128,8,128]{0,2,1:T(8,128)} %bitcast.48) | data formatting | bytes 1048576 | tf_op jit(solution)/shard_map/reshape | solution.py:48
  43.2 60.8 %all-gather.2.cloned.1.call-done = bf16[2,2048,8,128]{3,1,2,0:T(8,128)(2,1)} async-done(((bf16[2,128,8,128]{3,1,2,0:T(8,128)(2,1)}), bf16[2,2048,8,128]{3,1,2,0:T(8,128)(2,1)}) %all-gather.2.cloned.1.call-update) | async-done | bytes 8388624 | tf_op jit(solution)/shard_map/all_gather | solution.py:63
  104.0 0.0 copy-done.5
  104.0 0.0 copy-start.4
  104.0 8.3 %fusion = (f32[8,128]{1,0:T(8,128)S(1)}, f32[8,128,2048]{2,1,0:T(8,128)}) fusion(f32[8]{0:T(128)S(1)} %copy-done.5, pred[128,2048]{1,0:T(8,128)(4,1)S(1)} %iota_compare_fusion, bf16[2,2048,8,128]{3,1,2,0:T(8,128)(2,1)} %all-gather.2.cloned.1.call-done, f32[128,8,128]{2,0,1:T(8,128)} %copy.16, f32[128,8]{0,1:T(8,128)S(1)} %add_rsqrt_fusion), kind=kOutput, calls=%fused_computation.1 | convolution fusion | flops 545520640 | bytes 13377568 | tf_op jit(solution)/shard_map/jsg,isg->sji/dot_general | solution.py:66
  112.3 0.0 copy-done.4
  112.3 0.0 copy-start.3
  112.3 5.8 %fusion.23 = bf16[128,8,128]{0,2,1:T(8,128)(2,1)S(1)} fusion(f32[8,128,2048]{2,1,0:T(8,128)} %get-tuple-element.10, f32[8]{0:T(128)S(1)} %copy-done.5, pred[128,2048]{1,0:T(8,128)(4,1)S(1)} %iota_compare_fusion, bf16[2,2048,8,128]{3,1,2,0:T(8,128)(2,1)S(1)} %copy-done.4, f32[128,8]{0,1:T(8,128)S(1)} %bitcast.54), kind=kOutput, calls=%fused_computation.25 | convolution fusion | flops 545521664 | bytes 13111808 | tf_op jit(solution)/shard_map/hqk,khd->qhd/dot_general | solution.py:77
  118.1 0.0 copy-done.3
  118.1 2.7 %convolution_bitcast_fusion = f32[128,32,256]{2,0,1:T(8,128)} fusion(bf16[128,32,32]{0,2,1:T(8,128)(2,1)S(1)} %bitcast.51, bf16[32,32,256]{2,1,0:T(8,128)(2,1)S(1)} %copy-done.3), kind=kOutput, calls=%fused_computation.15 | convolution fusion | flops 67108864 | bytes 4980736 | tf_op jit(solution)/shard_map/jgc,gcu->jgu/dot_general | solution.py:85
  120.8 5.6 %copy.18 = f32[128,32,256]{0,2,1:T(8,128)} copy(f32[128,32,256]{2,0,1:T(8,128)} %convolution_bitcast_fusion) | data formatting | bytes 8388608 | tf_op jit(solution)/shard_map/jgc,gcu->jgu/transpose | solution.py:85
  126.4 9.1 %copy.19 = f32[128,4,32,64]{3,2,1,0:T(8,128)} copy(f32[128,4,32,64]{0,3,1,2:T(8,128)} %bitcast.46) | data formatting | bytes 8388608 | tf_op jit(solution)/shard_map/transpose | solution.py:90
  135.5 7.8 %reshape.99 = f32[512,2048]{1,0:T(8,128)} reshape(f32[128,4,32,64]{3,2,1,0:T(8,128)} %copy.19) | data formatting | bytes 8388608 | tf_op jit(solution)/shard_map/reshape | solution.py:91
  143.3 0.0 copy-start.1
  143.3 3.0 %multiply_reduce_fusion = f32[512]{0:T(512)S(1)} fusion(f32[512,2048]{1,0:T(8,128)} %reshape.99, bf16[512,2048]{1,0:T(8,128)(2,1)S(1)} %copy-done.2), kind=kLoop, calls=%fused_computation.10 | loop fusion | flops 4193792 | bytes 6293504 | tf_op jit(solution)/shard_map/reduce_sum | solution.py:94
  146.3 0.0 copy-done
  146.3 0.5 copy-done.1
  146.8 1.5 fusion.19
  (7 shorter events, 0.1 us)
Async XLA Ops:
  6.5 139.8 %copy-start = (bf16[256,2048]{1,0:T(8,128)(2,1)S(1)}, bf16[256,2048]{1,0:T(8,128)(2,1)}, u32[]{:S(2)}) copy-start(bf16[256,2048]{1,0:T(8,128)(2,1)} %param.6) | copy-start | bytes 3145732
  6.5 10.3 %copy-start.2 = (bf16[512,2048]{1,0:T(8,128)(2,1)S(1)}, bf16[512,2048]{1,0:T(8,128)(2,1)}, u32[]{:S(2)}) copy-start(bf16[512,2048]{1,0:T(8,128)(2,1)} %param.5) | copy-start | bytes 6291460
  6.5 97.4 %all-gather.2.cloned.1.call-start = ((), (), s32[]{:S(2)}) async-start(), calls=%async_computation | async-start | bytes 8912896 | tf_op jit(solution)/shard_map/all_gather | solution.py:63
  7.5 9.4 %collective-permute-start = (bf16[3,2048]{1,0:T(4,128)(2,1)S(1)}, bf16[3,2048]{1,0:T(4,128)(2,1)S(1)}, u32[]{:S(2)}, u32[]{:S(2)}) collective-permute-start(bf16[3,2048]{1,0:T(4,128)(2,1)S(1)} %slice.22), channel_id=1, source_target_pairs={{0,1},{1,2},{2,3},{3,4},{4,5},{5,6},{6,7},{7,8},{8,9},{9,10},{10,1... | collective-permute-start | bytes 36872 | tf_op jit(solution)/shard_map/ppermute | solution.py:12
  33.7 70.3 %copy-start.5 = (f32[8]{0:T(128)S(1)}, f32[8]{0:T(128)}, u32[]{:S(2)}) copy-start(f32[8]{0:T(128)} %param.8) | copy-start | bytes 100
  104.0 8.3 %copy-start.4 = (bf16[2,2048,8,128]{3,1,2,0:T(8,128)(2,1)S(1)}, bf16[2,2048,8,128]{3,1,2,0:T(8,128)(2,1)}, u32[]{:S(2)}) copy-start(bf16[2,2048,8,128]{3,1,2,0:T(8,128)(2,1)} %all-gather.2.cloned.1.call-done) | copy-start | bytes 25165828
  112.3 5.9 %copy-start.3 = (bf16[32,32,256]{2,1,0:T(8,128)(2,1)S(1)}, bf16[32,32,256]{2,1,0:T(8,128)(2,1)}, u32[]{:S(2)}) copy-start(bf16[32,32,256]{2,1,0:T(8,128)(2,1)} %param.9) | copy-start | bytes 1572868
  143.3 3.4 %copy-start.1 = (f32[512,2048]{1,0:T(8,128)S(1)}, f32[512,2048]{1,0:T(8,128)}, u32[]{:S(2)}) copy-start(f32[512,2048]{1,0:T(8,128)} %reshape.99) | copy-start | bytes 12582916
Sparse Core Ops, SparseCore 0:
  41.0 62.9 all-gather.1
where the time goes:
time: 156 us; the launch traced here: 155 us
  waiting for transfers between devices  60.8 us (39%)
  local copies, waits for them, and re-layouts  39.9 us (26%)
  matrix products  26.1 us (17%)
  between operations  13.5 us (9%)
  other arithmetic  9.4 us (6%)
  starting transfers between devices  5.51 us (4%)
    all_gather x1, waiting for transfers between devices, on_device(): gathered = lax.all_gather(stacked, 'seq', axis=1, tiled=True)  60.8 us
    transpose x1, local copies, waits for them, and re-layouts, on_device(): upsampled = upsampled.reshape(tokens_here, groups, SHORTEN, group_width)....  9.14 us
    dot_general x1, matrix products, on_device(): jnp.einsum('jsg,isg->sji', queries, all_keys, preferred_element_type=jnp....  8.29 us
    reshape x1, local copies, waits for them, and re-layouts, on_device(): upsampled = upsampled.reshape(tokens_here, groups, SHORTEN, group_width)....  7.82 us
    dot_general x1, matrix products, shorten(): jnp.einsum('jtgc,gtco->jgo', windows, kernel, preferred_element_type=jnp....  7.76 us
    reshape x1, local copies, waits for them, and re-layouts, shorten(): shifted.reshape(byte_rows // SHORTEN, SHORTEN, groups, model_width // gro...  7.08 us
    dot_general x1, matrix products, on_device(): jnp.einsum('hqk,khd->qhd', softmax_shares.astype(jnp.bfloat16), all_value...  5.85 us
    transpose x1, local copies, waits for them, and re-layouts, on_device(): jnp.einsum('jgc,gcu->jgu', attended, widening_filter, preferred_element_t...  5.56 us
  transfers between devices with their start and end apart: 2, of which 1 were waited for; matrix products, arithmetic and copies ran while one was open for 4% of the time, Pallas kernels for 0%

commit v1 on v0

--- a/solution.py
+++ b/solution.py
@@ -4,6 +4,16 @@
 from jax.sharding import PartitionSpec as P
 
 SHORTEN = 4
+
+
+def ladders_advance(array_in, join_dim=1):
+    back = jnp.concatenate(
+        lax.all_to_all(
+            jnp.stack([array_in] * lax.axis_size("seq"), 0), "seq", split_axis=0, concat_axis=0
+        ),
+        join_dim,
+    )
+    return back
 
 
 def shifted_2(array, axis, by):
@@ -60,7 +70,7 @@
     sharpness_vertical = sharpness_factor[:, None, None]
     query_pos = first_token + jnp.arange(tokens_here, dtype=jnp.int32)
     stacked = jnp.stack([key_unit, values], 0)
-    gathered = lax.all_gather(stacked, "seq", axis=1, tiled=True)
+    gathered = ladders_advance(stacked)
     all_keys, all_values = (gathered[0], gathered[1])
     similarity_matrix = (
         jnp.einsum("jsg,isg->sji", queries, all_keys, preferred_element_type=jnp.float32)

time: 156 us -> 291 us (1.87)
  waiting for transfers between devices: 60.8 us -> 181 us
  local copies, waits for them, and re-layouts: 39.9 us -> 68.1 us
  between operations: 13.5 us -> 0.14 us
  starting transfers between devices: 5.51 us -> 15 us
  matrix products: 26.1 us -> 17.1 us
    all_to_all x0 -> x1, waiting for transfers between devices: none -> 181 us  [ladders_advance(): lax.all_to_all(jnp.stack([array_in] * lax.axis_size('seq'), 0), 'seq', sp...]
    all_gather x1 -> x0, waiting for transfers between devices: 60.8 us -> none  [on_device(): gathered = lax.all_gather(stacked, 'seq', axis=1, tiled=True)]
    slice x0 -> x3, local copies, waits for them, and re-layouts: none -> 15.4 us  [on_device(): all_keys, all_values = (gathered[0], gathered[1])]
    all_to_all x0 -> x1, starting transfers between devices: none -> 9.53 us  [ladders_advance(): lax.all_to_all(jnp.stack([array_in] * lax.axis_size('seq'), 0), 'seq', sp...]
    another operation x0 -> x2, local copies, waits for them, and re-layouts: none -> 8.43 us  [the longest x1 6.39 us: ladders_advance(): jnp.stack([array_in] * lax.axis_size('seq'), 0)]
    squeeze x0 -> x1, local copies, waits for them, and re-layouts: none -> 7.31 us  [on_device(): all_keys, all_values = (gathered[0], gathered[1])]
    dot_general x1, matrix products: 8.29 us -> 3 us  [on_device(): jnp.einsum('jsg,isg->sji', queries, all_keys, preferred_element_type=jnp....]
    dot_general x1, matrix products: 5.85 us -> 2.14 us  [on_device(): jnp.einsum('hqk,khd->qhd', softmax_shares.astype(jnp.bfloat16), all_value...]
  transfers between devices with their start and end apart: 2 -> 2, of which waited for: 1 -> 1; matrix products, arithmetic and copies ran while one was open for 4% -> 2% of each run, Pallas kernels for 0% -> 0%
where the time goes in v1:
time: 291 us; the launch traced here: 290 us
  waiting for transfers between devices  181 us (62%)
  local copies, waits for them, and re-layouts  68.1 us (23%)
  matrix products  17.1 us (6%)
  starting transfers between devices  15 us (5%)
  other arithmetic  8.25 us (3%)
    all_to_all x1, waiting for transfers between devices, ladders_advance(): lax.all_to_all(jnp.stack([array_in] * lax.axis_size('seq'), 0), 'seq', sp...  181 us
    slice x3, local copies, waits for them, and re-layouts, on_device(): all_keys, all_values = (gathered[0], gathered[1])  15.4 us
    all_to_all x1, starting transfers between devices, ladders_advance(): lax.all_to_all(jnp.stack([array_in] * lax.axis_size('seq'), 0), 'seq', sp...  9.53 us
    transpose x1, local copies, waits for them, and re-layouts, on_device(): upsampled = upsampled.reshape(tokens_here, groups, SHORTEN, group_width)....  9.14 us
    reshape x1, local copies, waits for them, and re-layouts, on_device(): upsampled = upsampled.reshape(tokens_here, groups, SHORTEN, group_width)....  7.82 us
    dot_general x1, matrix products, shorten(): jnp.einsum('jtgc,gtco->jgo', windows, kernel, preferred_element_type=jnp....  7.76 us
    squeeze x1, local copies, waits for them, and re-layouts, on_device(): all_keys, all_values = (gathered[0], gathered[1])  7.31 us
    reshape x1, local copies, waits for them, and re-layouts, shorten(): shifted.reshape(byte_rows // SHORTEN, SHORTEN, groups, model_width // gro...  7.08 us
  transfers between devices with their start and end apart: 2, of which 1 were waited for; matrix products, arithmetic and copies ran while one was open for 2% of the time, Pallas kernels for 0%

profile of v1, /device:TPU:1, one launch (start us, length us, event | category | flops | bytes accessed | tf_op | source)
XLA Modules:
  0.0 289.7 jit_solution(10863437891994621171)
XLA Ops:
  0.0 0.0 copy-start
  0.0 0.0 copy-start.2
  0.0 0.9 slice.24
  0.9 5.5 %collective-permute-start = (bf16[3,2048]{1,0:T(4,128)(2,1)S(1)}, bf16[3,2048]{1,0:T(4,128)(2,1)S(1)}, u32[]{:S(2)}, u32[]{:S(2)}) collective-permute-start(bf16[3,2048]{1,0:T(4,128)(2,1)S(1)} %slice.24), channel_id=1, source_target_pairs={{0,1},{1,2},{2,3},{3,4},{4,5},{5,6},{6,7},{7,8},{8,9},{9,10},{10,1... | collective-permute-start | bytes 36872 | tf_op jit(solution)/shard_map/ppermute | solution.py:22
  6.4 3.9 %copy.18 = bf16[32,256,96]{2,1,0:T(8,128)(2,1)} copy(bf16[32,256,96]{1,2,0:T(8,128)(2,1)} %param.7) | data formatting | bytes 3145728 | tf_op args[2]
  10.3 0.0 collective-permute-done
  10.3 0.0 copy-done.2
  10.3 1.9 pad_maximum_fusion
  12.3 7.1 %reshape.103 = bf16[128,4,32,64]{3,2,1,0:T(8,128)(2,1)} reshape(bf16[512,2048]{1,0:T(8,128)(2,1)} %pad_maximum_fusion) | data formatting | bytes 4194304 | tf_op jit(solution)/shard_map/reshape | solution.py:37
  19.3 7.8 %fusion.11 = f32[128,32,96]{0,2,1:T(8,128)S(1)} fusion(bf16[32,4,64,96]{3,2,1,0:T(8,128)(2,1)} %bitcast.42, bf16[128,4,32,64]{3,2,1,0:T(8,128)(2,1)} %reshape.103), kind=kOutput, calls=%fused_computation.16 | convolution fusion | flops 201326592 | bytes 5242880 | tf_op jit(solution)/shard_map/jtgc,gtco->jgo/dot_general | solution.py:39
  27.2 1.2 multiply_reduce_fusion.1
  28.3 1.1 multiply_convert_fusion.7
  29.4 0.8 pad_maximum_fusion.1
  30.3 2.0 copy.20
  32.3 6.4 %stack.5 = bf16[16,2,128,8,128]{4,2,3,1,0:T(8,128)(2,1)} broadcast(bf16[2,128,8,128]{3,1,2,0:T(8,128)(2,1)} %copy.20), dimensions={1,2,3,4} | broadcast | bytes 8912896 | tf_op jit(solution)/shard_map/stack | solution.py:12
  38.7 9.5 %all-to-all-start = ((bf16[16,2,128,8,128]{4,2,3,1,0:T(8,128)(2,1)}), bf16[16,2,128,8,128]{4,2,3,1,0:T(8,128)(2,1)}, u32[]{:S(2)}, u32[]{:S(2)}) async-start(bf16[16,2,128,8,128]{4,2,3,1,0:T(8,128)(2,1)} %stack.5), calls=%async_computation | async-start | bytes 16777216 | tf_op jit(solution)/shard_map/all_to_all | solution.py:11
  48.2 0.2 iota_compare_fusion
  48.5 2.0 copy.22
  50.5 181.1 %all-to-all-done = bf16[16,2,128,8,128]{4,2,3,1,0:T(8,128)(2,1)} async-done(((bf16[16,2,128,8,128]{4,2,3,1,0:T(8,128)(2,1)}), bf16[16,2,128,8,128]{4,2,3,1,0:T(8,128)(2,1)}, u32[]{:S(2)}, u32[]{:S(2)}) %all-to-all-start) | async-done | bytes 8388640 | tf_op jit(solution)/shard_map/all_to_all | solution.py:11
  231.6 6.0 %fusion.28 = (bf16[1,16,128,8,128]{4,2,3,0,1:T(8,128)(2,1)}, bf16[1,16,128,8,128]{4,2,3,0,1:T(8,128)(2,1)}) fusion(bf16[2,16,128,8,128]{4,2,3,0,1:T(8,128)(2,1)} %bitcast.8), kind=kLoop, calls=%fused_computation.36 | loop fusion | bytes 16777216 | tf_op jit(solution)/shard_map/slice | solution.py:74
  237.7 6.8 %copy.21 = bf16[1,16,128,8,128]{2,1,4,3,0:T(8,128)(2,1)} copy(bf16[1,16,128,8,128]{4,2,3,0,1:T(8,128)(2,1)} %get-tuple-element.8) | data formatting | bytes 8388608 | tf_op jit(solution)/shard_map/slice | solution.py:74
  244.4 7.3 %squeeze.6 = bf16[2048,8,128]{0,2,1:T(8,128)(2,1)} reshape(bf16[1,16,128,8,128]{2,1,4,3,0:T(8,128)(2,1)} %copy.21) | data formatting | bytes 8388608 | tf_op jit(solution)/shard_map/squeeze | solution.py:74
  251.8 0.0 copy-start.5
  251.8 0.0 copy-start.6
  251.8 2.6 copy.23
  254.3 0.0 copy-done.5
  254.3 0.0 copy-done.6
  254.3 0.0 copy-start.3
  254.4 3.0 %fusion = (f32[8,128]{1,0:T(8,128)S(1)}, f32[8,128,2048]{2,1,0:T(8,128)S(1)}) fusion(f32[8]{0:T(128)S(1)} %copy-done.6, pred[128,2048]{1,0:T(8,128)(4,1)S(1)} %iota_compare_fusion, bf16[2048,8,128]{2,0,1:T(8,128)(2,1)S(1)} %bitcast.41, f32[128,8,128]{2,0,1:T(8,128)S(1)} %copy-done.5, f32[128,8]{0,1:T(8,128)S(1)} %add_rsqrt_fusion), kind=kOutput, calls=%fused_computation.1 | convolution fusion | flops 545520640 | bytes 13377568 | tf_op jit(solution)/shard_map/jsg,isg->sji/dot_general | solution.py:76
  257.4 0.0 copy-done.3
  257.4 0.0 copy-start.4
  257.4 2.1 fusion.22
  259.5 0.0 copy-done.4
  259.5 2.7 convolution_bitcast_fusion
  262.2 5.6 %copy.24 = f32[128,32,256]{0,2,1:T(8,128)} copy(f32[128,32,256]{2,0,1:T(8,128)} %convolution_bitcast_fusion) | data formatting | bytes 8388608 | tf_op jit(solution)/shard_map/jgc,gcu->jgu/transpose | solution.py:95
  267.8 9.1 %copy.25 = f32[128,4,32,64]{3,2,1,0:T(8,128)} copy(f32[128,4,32,64]{0,3,1,2:T(8,128)} %bitcast.40) | data formatting | bytes 8388608 | tf_op jit(solution)/shard_map/transpose | solution.py:100
  276.9 7.8 %reshape.110 = f32[512,2048]{1,0:T(8,128)} reshape(f32[128,4,32,64]{3,2,1,0:T(8,128)} %copy.25) | data formatting | bytes 8388608 | tf_op jit(solution)/shard_map/reshape | solution.py:101
  284.7 0.0 copy-start.1
  284.7 3.0 %multiply_reduce_fusion = f32[512]{0:T(512)S(1)} fusion(f32[512,2048]{1,0:T(8,128)} %reshape.110, bf16[512,2048]{1,0:T(8,128)(2,1)S(1)} %copy-done.2), kind=kLoop, calls=%fused_computation.7 | loop fusion | flops 4193792 | bytes 6293504 | tf_op jit(solution)/shard_map/reduce_sum | solution.py:104
  287.7 0.0 copy-done
  287.7 0.5 copy-done.1
  288.2 1.5 fusion.18
  (7 shorter events, 0.1 us)
Async XLA Ops:
  0.0 287.7 %copy-start = (bf16[256,2048]{1,0:T(8,128)(2,1)S(1)}, bf16[256,2048]{1,0:T(8,128)(2,1)}, u32[]{:S(2)}) copy-start(bf16[256,2048]{1,0:T(8,128)(2,1)} %param.6) | copy-start | bytes 3145732
  0.0 10.3 %copy-start.2 = (bf16[512,2048]{1,0:T(8,128)(2,1)S(1)}, bf16[512,2048]{1,0:T(8,128)(2,1)}, u32[]{:S(2)}) copy-start(bf16[512,2048]{1,0:T(8,128)(2,1)} %param.5) | copy-start | bytes 6291460
  0.9 9.4 %collective-permute-start = (bf16[3,2048]{1,0:T(4,128)(2,1)S(1)}, bf16[3,2048]{1,0:T(4,128)(2,1)S(1)}, u32[]{:S(2)}, u32[]{:S(2)}) collective-permute-start(bf16[3,2048]{1,0:T(4,128)(2,1)S(1)} %slice.24), channel_id=1, source_target_pairs={{0,1},{1,2},{2,3},{3,4},{4,5},{5,6},{6,7},{7,8},{8,9},{9,10},{10,1... | collective-permute-start | bytes 36872 | tf_op jit(solution)/shard_map/ppermute | solution.py:22
  38.7 192.9 %all-to-all-start = ((bf16[16,2,128,8,128]{4,2,3,1,0:T(8,128)(2,1)}), bf16[16,2,128,8,128]{4,2,3,1,0:T(8,128)(2,1)}, u32[]{:S(2)}, u32[]{:S(2)}) async-start(bf16[16,2,128,8,128]{4,2,3,1,0:T(8,128)(2,1)} %stack.5), calls=%async_computation | async-start | bytes 16777216 | tf_op jit(solution)/shard_map/all_to_all | solution.py:11
  251.8 2.6 copy-start.5
  251.8 2.6 copy-start.6
  254.3 3.0 %copy-start.3 = (bf16[2048,8,128]{0,2,1:T(8,128)(2,1)S(1)}, bf16[2048,8,128]{0,2,1:T(8,128)(2,1)}, u32[]{:S(2)}) copy-start(bf16[2048,8,128]{0,2,1:T(8,128)(2,1)} %squeeze.6) | copy-start | bytes 12582916
  257.4 2.2 copy-start.4
  284.7 3.4 %copy-start.1 = (f32[512,2048]{1,0:T(8,128)S(1)}, f32[512,2048]{1,0:T(8,128)}, u32[]{:S(2)}) copy-start(f32[512,2048]{1,0:T(8,128)} %reshape.110) | copy-start | bytes 12582916
